TPU v7x, 512 devices: a whole 4x4x16 slice. The times are simulated.
512 devices in a mesh: mem: 128 (over x, z, core), rep: 4 (over y).
Axes of the slice: x: 4, y: 4, z: 16, core: 2. Of those that a mesh axis runs over, the one named last changes fastest.
Arguments:
- states: bfloat16 [2048, 384], P('rep'), may hold values from -6 to 6
- batch_index: int32 [2, 2048], P(None, 'rep'), may hold values from 0 to 511
- obs_pick: int32 [2, 128], replicated, may hold values from 0 to 383
- norm_gain: float32 [384], replicated, may hold values from 0.5 to 1.5
- w_in: bfloat16 [384, 1024], replicated, may hold values from -0.3125 to 0.3125
- b_in: float32 [1024], replicated, may hold values from -0.5 to 0.5
- member_params: bfloat16 [128, 393216], P('mem', 'rep'), may hold values from -6 to 6
- observed: bfloat16 [2, 2048, 128], P(None, 'rep'), may hold values from -6 to 6
- perturbation: bfloat16 [128, 2, 2048, 128], P('mem', None, 'rep'), may hold values from -6 to 6
- inv_sigma: float32 [2, 2048, 128], P(None, 'rep'), may hold values from 0.5 to 4
Outputs:
- updated_params: bfloat16 [128, 393216], P('mem', 'rep')
Inputs may be any that keep to these rules, and one draw needn't show every extreme that they name: `batch_index`: row number of a start state inside the block of 512 given states that belongs to its block of 512 batch rows. `obs_pick`: observed feature numbers; a number may repeat.
All inputs are finite; a program needn't handle non-finite values.
Results may differ from a plain program's by a relative error of at most 0.0056.
Values may be sent and summed in bfloat16 or wider, within the bound.
No kernel may reach another device: no remote copies, remote signals or barrier semaphores. Data moves between devices by JAX's collectives and lax.ppermute only.
A program may use at most 64 MiB of HBM per device.

v0:
```python
import jax
import jax.numpy as jnp
from jax import lax
from jax.sharding import PartitionSpec as P

EPS = 1e-06
DT = 0.5


def hidden_layer(state, norm_gain, w_in, b_in):
    normed = (
        state * lax.rsqrt(jnp.mean(state * state, axis=-1, keepdims=True) + EPS) * norm_gain
    ).astype(jnp.bfloat16)
    return jax.nn.gelu(jnp.dot(normed, w_in, preferred_element_type=jnp.float32) + b_in).astype(
        jnp.bfloat16
    )


def member_sums(pieces):
    weighted, misfit_w = pieces
    count = weighted.shape[0]
    gram_list = []
    innov_list = []
    for item_index in range(weighted.shape[1]):
        flat = weighted[:, item_index].reshape(count, -1).astype(jnp.float32)
        anomaly = (flat - jnp.mean(flat, axis=0)).astype(jnp.bfloat16)
        misfit_flat = misfit_w[:, item_index].reshape(count, -1)
        gram_list.append(
            lax.dot_general(
                anomaly, anomaly, (((1,), (1,)), ((), ())), preferred_element_type=jnp.float32
            )
        )
        innov_list.append(
            lax.dot_general(
                anomaly, misfit_flat, (((1,), (1,)), ((), ())), preferred_element_type=jnp.float32
            )
        )
    return (jnp.stack(gram_list, axis=0), jnp.stack(innov_list, axis=0))


def solve_columns(system, right_side):
    lower_factor = jnp.linalg.cholesky(system)
    halfway = lax.linalg.triangular_solve(lower_factor, right_side, left_side=True, lower=True)
    return lax.linalg.triangular_solve(
        lower_factor, halfway, left_side=True, lower=True, transpose_a=True
    )


def on_device(
    states,
    batch_index,
    obs_pick,
    norm_gain,
    w_in,
    b_in,
    member_params,
    observed,
    perturbation,
    inv_sigma,
):
    local_members = member_params.shape[0]
    width = w_in.shape[1]
    features = w_in.shape[0]
    step_count = batch_index.shape[0]
    picked = obs_pick.shape[1]
    whole_params = lax.all_gather(member_params, "rep", axis=1, tiled=True)
    weights = whole_params.reshape(local_members, width, features)
    step_scale = DT * width ** (-0.5)
    start_state = jnp.take(states, batch_index, axis=0).astype(jnp.float32)
    shared = hidden_layer(start_state, norm_gain, w_in, b_in)
    current = start_state[None] + step_scale * jnp.einsum(
        "kbh,jhs->jkbs", shared, weights, preferred_element_type=jnp.float32
    )
    layer = hidden_layer(current, norm_gain, w_in, b_in)
    current = current + step_scale * jnp.einsum(
        "jkbh,jhs->jkbs", layer, weights, preferred_element_type=jnp.float32
    )
    feature_ids = lax.broadcasted_iota(jnp.int32, (step_count, features, picked), 1)
    selector = (feature_ids == obs_pick[:, None, :]).astype(jnp.float32)
    predicted = jnp.einsum("jkbs,ksf->jkbf", current, selector, precision=lax.Precision.HIGHEST)
    weighted = (predicted * inv_sigma).astype(jnp.bfloat16)
    misfit_w = (
        observed.astype(jnp.float32) * inv_sigma
        + perturbation.astype(jnp.float32)
        - predicted * inv_sigma
    ).astype(jnp.bfloat16)
    misfit_local = jnp.sum(jnp.square(misfit_w.astype(jnp.float32)))
    gram_items, innov_items = member_sums(
        (
            lax.all_to_all(weighted, "mem", split_axis=2, concat_axis=0, tiled=True),
            lax.all_to_all(misfit_w, "mem", split_axis=2, concat_axis=0, tiled=True),
        )
    )
    gram_matrix = jnp.sum(gram_items, axis=0)
    innovation = jnp.sum(innov_items, axis=0)
    members = gram_matrix.shape[0]
    entries = members * step_count * batch_index.shape[1] * lax.axis_size("rep") * picked
    identity = jnp.eye(members, dtype=jnp.float32)
    gram_matrix, innovation, misfit_total = lax.psum(
        (gram_matrix, innovation, misfit_local), ("mem", "rep")
    )
    system = gram_matrix + (1.0 + misfit_total / entries) * (members - 1) * identity
    coefficients = solve_columns(system, innovation)
    param_block = lax.all_to_all(member_params, "mem", split_axis=1, concat_axis=0, tiled=True)
    params_f = param_block.astype(jnp.float32)
    spread = params_f - jnp.mean(params_f, axis=0)
    change = jnp.einsum("kj,kp->jp", coefficients, spread, precision=lax.Precision.HIGHEST)
    renewed = (params_f + change).astype(jnp.bfloat16)
    return lax.all_to_all(renewed, "mem", split_axis=0, concat_axis=1, tiled=True)


def solution(mesh):
    placed = (
        P("rep", None),
        P(None, "rep"),
        P(),
        P(),
        P(),
        P(),
        P("mem", "rep"),
        P(None, "rep", None),
        P("mem", None, "rep", None),
        P(None, "rep", None),
    )
    return jax.shard_map(
        on_device, mesh=mesh, in_specs=placed, out_specs=P("mem", "rep"), check_vma=False
    )
```

profile of v0, /device:TPU:8, one launch (start us, length us, event | category | flops | bytes accessed | tf_op | source)
XLA Modules:
  0.0 755.3 jit_solution(18304707724078509563)
XLA Ops:
  6.5 0.0 copy-start
  6.5 0.0 copy-start.2
  6.5 0.6 broadcast.183
  7.1 2.8 reduce.16
  9.9 0.7 reshape.213
  10.6 20.2 %all-to-all-start = ((bf16[128,2,384]{2,1,0:T(2,128)(2,1)}), bf16[128,2,384]{2,1,0:T(2,128)(2,1)}, u32[]{:S(2)}, u32[]{:S(2)}) async-start(bf16[128,2,384]{2,1,0:T(2,128)(2,1)} %reshape.213), calls=%async_computation | async-start | bytes 393216 | tf_op jit(solution)/shard_map/all_to_all | solution.py:104
  30.9 0.7 fusion.75
  31.5 0.7 compare_and_fusion
  32.2 0.0 copy-done.2
  32.2 17.5 %all_gather.3 = bf16[1,393216]{1,0:T(2,128)(2,1)S(1)} all-gather(bf16[1,98304]{1,0:T(2,128)(2,1)S(1)} %copy-done.2), channel_id=1, replica_groups=mesh['mem'=128,'rep'=4] {'rep'}, dimensions={1}, use_global_device_ids=true | all-gather | bytes 983040 | tf_op jit(solution)/shard_map/all_gather | solution.py:66
  49.8 16.3 %reduce.14 = bf16[393216]{0:T(1024)(128)(2,1)S(1)} reduce(bf16[1,393216]{1,0:T(2,128)(2,1)S(1)} %all_gather.3, bf16[]{:T(256)} %constant.98), dimensions={0}, to_apply=%all_gather.3.reduce_sub_computation | reduce | bytes 1572866 | tf_op jit(solution)/shard_map/all_gather | solution.py:66
  66.1 0.0 copy-start.1
  66.1 1.2 reshape.185
  67.4 1.3 reshape.205
  68.6 0.0 copy-done.1
  68.6 4.1 gather_fusion
  72.7 0.0 copy-start.5
  72.7 0.0 copy-start.6
  72.8 0.4 fusion.16
  73.2 1.2 copy.38
  74.4 0.0 copy-done
  74.4 0.0 copy-done.5
  74.4 0.0 copy-done.6
  74.4 0.0 copy-start.3
  74.4 4.1 multiply_reduce_fusion
  78.6 1.2 copy.43
  79.9 0.0 copy-done.3
  79.9 0.1 copy.50
  80.0 1.8 copy.52
  81.8 5.2 fusion.25
  87.0 0.0 copy-done.4
  87.0 3.7 multiply_reduce_fusion.1
  90.7 1.8 copy.44
  92.5 0.0 all-to-all-done
  92.5 16.3 %all-to-all-start.1 = ((bf16[1,2,512,128]{3,1,0,2:T(2,128)(2,1)}), bf16[1,2,512,128]{3,1,0,2:T(2,128)(2,1)S(1)}, u32[]{:S(2)}, u32[]{:S(2)}) async-start(bf16[1,2,512,128]{3,1,0,2:T(2,128)(2,1)} %copy.44), calls=%async_computation.1 | async-start | bytes 524288 | tf_op jit(solution)/shard_map/all_to_all | solution.py:90
  108.8 0.9 copy.54
  109.7 22.9 %all-to-all-done.1 = bf16[1,2,512,128]{3,1,0,2:T(2,128)(2,1)S(1)} async-done(((bf16[1,2,512,128]{3,1,0,2:T(2,128)(2,1)}), bf16[1,2,512,128]{3,1,0,2:T(2,128)(2,1)S(1)}, u32[]{:S(2)}, u32[]{:S(2)}) %all-to-all-start.1) | async-done | bytes 262176 | tf_op jit(solution)/shard_map/all_to_all | solution.py:90
  132.6 6.2 all-to-all-start.2
  138.7 0.0 all-reduce.3.cloned.1.call-start
  138.8 105.2 %psum.22 = f32[]{:T(128)} all-reduce(f32[]{:T(128)} %get-tuple-element.9), channel_id=1, replica_groups=mesh['mem'=128,'rep'=4] {'mem','rep'}, use_global_device_ids=true, to_apply=%region_6.7 | all-reduce | flops 1 | bytes 8 | tf_op jit(solution)/shard_map/psum | solution.py:99
  244.6 1.6 reshape.214
  246.3 0.1 convert_reduce_fusion.2
  246.5 0.1 fusion.63
  246.6 0.2 convolution_bitcast_fusion.2
  246.8 0.0 all-to-all-done.2
  246.8 0.2 convolution_bitcast_fusion
  247.0 0.8 fusion.31
  247.8 0.8 fusion.32
  248.7 0.0 all-reduce.3.cloned.1.call-update
  248.7 442.5 %all-reduce.3.cloned.1.call-done = (f32[128,128]{1,0:T(8,128)}, f32[128,128]{1,0:T(8,128)}) async-done(((f32[128,128]{1,0:T(8,128)}, f32[128,128]{1,0:T(8,128)}), (f32[128,128]{1,0:T(8,128)}, f32[128,128]{1,0:T(8,128)})) %all-reduce.3.cloned.1.call-update) | async-done | bytes 131088 | tf_op jit(solution)/shard_map/psum | solution.py:99
  691.2 0.9 select_add_fusion
  692.1 0.1 copy.53
  692.2 0.9 fusion.74
  693.0 11.7 %cholesky.16 = f32[128,128]{1,0:T(8,128)S(1)} custom-call(f32[128,128]{1,0:T(8,128)S(1)} %fusion.74), custom_call_target="Cholesky" | custom-call | tf_op jit(solution)/shard_map/jit(cholesky)/cholesky | solution.py:42
  704.8 0.6 compare_reduce_fusion
  705.4 0.7 fusion.69
  706.1 9.8 %custom-call.8 = f32[1,128,128]{1,2,0:T(8,128)S(1)} custom-call(f32[1,128,128]{2,1,0:T(8,128)S(1)} %fusion.69), custom_call_target="InvertDiagBlocksLowerTriangular" | custom-call | tf_op jit(solution)/shard_map/triangular_solve | solution.py:44
  715.9 1.1 fusion.72
  717.0 0.2 fusion.70
  717.2 0.5 fusion.30
  717.8 0.8 reduce.17
  718.5 0.1 reshape.215
  718.6 28.9 %all_to_all.65 = bf16[128,2,384]{2,1,0:T(2,128)(2,1)S(1)} all-to-all(bf16[128,2,384]{2,1,0:T(2,128)(2,1)S(1)} %reshape.215), channel_id=1, replica_groups=mesh['mem'=128,'rep'=4] {'mem'}, dimensions={0} | all-to-all | bytes 393216 | tf_op jit(solution)/shard_map/all_to_all | solution.py:109
  747.5 0.9 reshape.216
  (11 shorter events, 0.2 us)
Async XLA Ops:
  6.5 67.9 %copy-start = (bf16[384,1024]{1,0:T(8,128)(2,1)S(1)}, bf16[384,1024]{1,0:T(8,128)(2,1)}, u32[]{:S(2)}) copy-start(bf16[384,1024]{1,0:T(8,128)(2,1)} %param.14) | copy-start | bytes 2359300
  6.5 25.7 %copy-start.2 = (bf16[1,98304]{1,0:T(2,128)(2,1)S(1)}, bf16[1,98304]{1,0:T(2,128)(2,1)}, u32[]{:S(2)}) copy-start(bf16[1,98304]{1,0:T(2,128)(2,1)} %param.16) | copy-start | bytes 589828
  10.6 81.9 %all-to-all-start = ((bf16[128,2,384]{2,1,0:T(2,128)(2,1)}), bf16[128,2,384]{2,1,0:T(2,128)(2,1)}, u32[]{:S(2)}, u32[]{:S(2)}) async-start(bf16[128,2,384]{2,1,0:T(2,128)(2,1)} %reshape.213), calls=%async_computation | async-start | bytes 393216 | tf_op jit(solution)/shard_map/all_to_all | solution.py:104
  66.1 2.5 copy-start.1
  72.7 1.7 copy-start.5
  72.7 1.7 copy-start.6
  74.4 5.4 copy-start.3
  81.8 5.2 copy-start.4
  92.5 40.0 %all-to-all-start.1 = ((bf16[1,2,512,128]{3,1,0,2:T(2,128)(2,1)}), bf16[1,2,512,128]{3,1,0,2:T(2,128)(2,1)S(1)}, u32[]{:S(2)}, u32[]{:S(2)}) async-start(bf16[1,2,512,128]{3,1,0,2:T(2,128)(2,1)} %copy.44), calls=%async_computation.1 | async-start | bytes 524288 | tf_op jit(solution)/shard_map/all_to_all | solution.py:90
  132.6 114.2 %all-to-all-start.2 = ((bf16[1,2,512,128]{3,1,0,2:T(2,128)(2,1)}), bf16[1,2,512,128]{3,1,0,2:T(2,128)(2,1)S(1)}, u32[]{:S(2)}, u32[]{:S(2)}) async-start(bf16[1,2,512,128]{3,1,0,2:T(2,128)(2,1)} %copy.54), calls=%async_computation.2 | async-start | bytes 524288 | tf_op jit(solution)/shard_map/all_to_all | solution.py:91
  138.7 552.5 %all-reduce.3.cloned.1.call-start = ((), (), s32[]{:S(2)}) async-start(), calls=%async_computation.4 | async-start | bytes 262144 | tf_op jit(solution)/shard_map/psum | solution.py:99
Sparse Core Ops, SparseCore 0:
  248.8 442.3 all-reduce.2
where the time goes:
time: 756 us; the launch traced here: 755 us
  waiting for transfers between devices  465 us (62%)
  blocking collectives  152 us (20%)
  other arithmetic  46.5 us (6%)
  starting transfers between devices  42.8 us (6%)
  local copies, waits for them, and re-layouts  17.6 us (2%)
  matrix products  16.9 us (2%)
  between operations  14.3 us (2%)
    psum x1, waiting for transfers between devices, on_device(): lax.psum((gram_matrix, innovation, misfit_local), ('mem', 'rep'))  443 us
    psum x1, blocking collectives, on_device(): lax.psum((gram_matrix, innovation, misfit_local), ('mem', 'rep'))  105 us
    all_to_all x1, blocking collectives, on_device(): lax.all_to_all(renewed, 'mem', split_axis=0, concat_axis=1, tiled=True)  28.9 us
    all_to_all x1, waiting for transfers between devices, on_device(): lax.all_to_all(weighted, 'mem', split_axis=2, concat_axis=0, tiled=True)  22.9 us
    all_to_all x1, starting transfers between devices, on_device(): lax.all_to_all(member_params, 'mem', split_axis=1, concat_axis=0, tiled=T...  20.2 us
    all_gather x1, blocking collectives, on_device(): whole_params = lax.all_gather(member_params, 'rep', axis=1, tiled=True)  17.5 us
    all_gather x1, other arithmetic, on_device(): whole_params = lax.all_gather(member_params, 'rep', axis=1, tiled=True)  16.3 us
    all_to_all x1, starting transfers between devices, on_device(): lax.all_to_all(weighted, 'mem', split_axis=2, concat_axis=0, tiled=True)  16.3 us
  transfers between devices with their start and end apart: 4, of which 2 were waited for; matrix products, arithmetic and copies ran while one was open for 6% of the time, Pallas kernels for 0%

commit v1 on v0

--- a/solution.py
+++ b/solution.py
@@ -97,7 +97,7 @@
     entries = members * step_count * batch_index.shape[1] * lax.axis_size("rep") * picked
     identity = jnp.eye(members, dtype=jnp.float32)
     gram_matrix, innovation, misfit_total = lax.psum(
-        (gram_matrix, innovation, misfit_local), ("mem", "rep")
+        lax.psum((gram_matrix, innovation, misfit_local), "mem"), "rep"
     )
     system = gram_matrix + (1.0 + misfit_total / entries) * (members - 1) * identity
     coefficients = solve_columns(system, innovation)

time: 756 us -> 838 us (1.11)
  the two profiles are of different devices: /device:TPU:8 before, /device:TPU:1 now
where the time goes in v1:
time: 838 us; the launch traced here: 837 us
  waiting for transfers between devices  379 us (45%)
  blocking collectives  316 us (38%)
  starting transfers between devices  46.7 us (6%)
  other arithmetic  46.5 us (6%)
  local copies, waits for them, and re-layouts  17.7 us (2%)
  matrix products  16.9 us (2%)
  between operations  14.3 us (2%)
    psum x1, waiting for transfers between devices, on_device(): lax.psum((gram_matrix, innovation, misfit_local), 'mem')  308 us
    psum x1, blocking collectives, on_device(): lax.psum((gram_matrix, innovation, misfit_local), 'mem')  253 us
    psum x1, waiting for transfers between devices, on_device(): lax.psum(lax.psum((gram_matrix, innovation, misfit_local), 'mem'), 'rep')  49.9 us
    all_to_all x1, blocking collectives, on_device(): lax.all_to_all(renewed, 'mem', split_axis=0, concat_axis=1, tiled=True)  38.4 us
    all_to_all x1, waiting for transfers between devices, on_device(): lax.all_to_all(weighted, 'mem', split_axis=2, concat_axis=0, tiled=True)  21.6 us
    all_to_all x1, starting transfers between devices, on_device(): lax.all_to_all(member_params, 'mem', split_axis=1, concat_axis=0, tiled=T...  20.8 us
    all_to_all x1, starting transfers between devices, on_device(): lax.all_to_all(weighted, 'mem', split_axis=2, concat_axis=0, tiled=True)  18.6 us
  transfers between devices with their start and end apart: 5, of which 3 were waited for; matrix products, arithmetic and copies ran while one was open for 6% of the time, Pallas kernels for 0%

profile of v1, /device:TPU:1, one launch (start us, length us, event | category | flops | bytes accessed | tf_op | source)
XLA Modules:
  0.0 837.3 jit_solution(652323702125672614)
XLA Ops:
  6.5 0.0 copy-start
  6.5 0.6 broadcast.183
  7.1 2.8 reduce.16
  9.9 0.7 reshape.213
  10.6 20.8 %all-to-all-start = ((bf16[128,2,384]{2,1,0:T(2,128)(2,1)}), bf16[128,2,384]{2,1,0:T(2,128)(2,1)}, u32[]{:S(2)}, u32[]{:S(2)}) async-start(bf16[128,2,384]{2,1,0:T(2,128)(2,1)} %reshape.213), calls=%async_computation | async-start | bytes 393216 | tf_op jit(solution)/shard_map/all_to_all | solution.py:104
  31.4 0.7 fusion.75
  32.1 0.7 compare_and_fusion
  32.8 0.0 copy-done.2
  32.8 16.5 %all_gather.3 = bf16[1,393216]{1,0:T(2,128)(2,1)S(1)} all-gather(bf16[1,98304]{1,0:T(2,128)(2,1)S(1)} %copy-done.2), channel_id=1, replica_groups=mesh['mem'=128,'rep'=4] {'rep'}, dimensions={1}, use_global_device_ids=true | all-gather | bytes 983040 | tf_op jit(solution)/shard_map/all_gather | solution.py:66
  49.3 16.3 %reduce.14 = bf16[393216]{0:T(1024)(128)(2,1)S(1)} reduce(bf16[1,393216]{1,0:T(2,128)(2,1)S(1)} %all_gather.3, bf16[]{:T(256)} %constant.98), dimensions={0}, to_apply=%all_gather.3.reduce_sub_computation | reduce | bytes 1572866 | tf_op jit(solution)/shard_map/all_gather | solution.py:66
  65.6 0.0 copy-start.1
  65.6 1.2 reshape.185
  66.9 1.3 reshape.205
  68.1 0.0 copy-done.1
  68.1 4.1 gather_fusion
  72.2 0.0 copy-start.5
  72.2 0.0 copy-start.6
  72.2 0.4 fusion.16
  72.7 1.2 copy.38
  73.9 0.0 copy-done
  73.9 4.1 multiply_reduce_fusion
  78.0 0.0 copy-start.3
  78.1 1.3 copy.43
  79.3 1.1 copy.50
  80.5 0.9 copy.52
  81.3 5.2 fusion.25
  86.5 0.0 copy-done.4
  86.5 3.7 multiply_reduce_fusion.1
  90.2 1.8 copy.44
  92.0 0.0 all-to-all-done
  92.0 18.6 %all-to-all-start.1 = ((bf16[1,2,512,128]{3,1,0,2:T(2,128)(2,1)}), bf16[1,2,512,128]{3,1,0,2:T(2,128)(2,1)S(1)}, u32[]{:S(2)}, u32[]{:S(2)}) async-start(bf16[1,2,512,128]{3,1,0,2:T(2,128)(2,1)} %copy.44), calls=%async_computation.1 | async-start | bytes 524288 | tf_op jit(solution)/shard_map/all_to_all | solution.py:90
  110.6 0.9 copy.54
  111.5 21.6 %all-to-all-done.1 = bf16[1,2,512,128]{3,1,0,2:T(2,128)(2,1)S(1)} async-done(((bf16[1,2,512,128]{3,1,0,2:T(2,128)(2,1)}), bf16[1,2,512,128]{3,1,0,2:T(2,128)(2,1)S(1)}, u32[]{:S(2)}, u32[]{:S(2)}) %all-to-all-start.1) | async-done | bytes 262176 | tf_op jit(solution)/shard_map/all_to_all | solution.py:90
  133.1 7.3 all-to-all-start.2
  140.4 0.0 all-reduce.5.cloned.1.call-start
  140.5 253.2 %psum.44 = f32[]{:T(128)} all-reduce(f32[]{:T(128)} %get-tuple-element.11), channel_id=1, replica_groups=mesh['mem'=128,'rep'=4] {'mem'}, use_global_device_ids=true, to_apply=%region_7.8 | all-reduce | flops 1 | bytes 8 | tf_op jit(solution)/shard_map/psum | solution.py:100
  393.7 8.0 psum.45
  402.3 1.6 reshape.214
  403.9 0.1 convert_reduce_fusion.2
  404.0 0.1 fusion.63
  404.2 0.2 convolution_bitcast_fusion.2
  404.4 0.0 all-to-all-done.2
  404.4 0.2 convolution_bitcast_fusion
  404.6 0.8 fusion.31
  405.4 0.8 fusion.32
  406.2 0.0 all-reduce.5.cloned.1.call-update
  406.3 0.0 all-reduce.7.cloned.1.call-start
  406.4 307.6 %all-reduce.5.cloned.1.call-done = (f32[128,128]{1,0:T(8,128)}, f32[128,128]{1,0:T(8,128)}) async-done(((f32[128,128]{1,0:T(8,128)}, f32[128,128]{1,0:T(8,128)}), (f32[128,128]{1,0:T(8,128)}, f32[128,128]{1,0:T(8,128)})) %all-reduce.5.cloned.1.call-update) | async-done | bytes 131088 | tf_op jit(solution)/shard_map/psum | solution.py:100
  714.0 0.0 all-reduce.7.cloned.1.call-update
  714.0 49.9 %all-reduce.7.cloned.1.call-done = (f32[128,128]{1,0:T(8,128)}, f32[128,128]{1,0:T(8,128)}) async-done(((f32[128,128]{1,0:T(8,128)}, f32[128,128]{1,0:T(8,128)}), (f32[128,128]{1,0:T(8,128)}, f32[128,128]{1,0:T(8,128)})) %all-reduce.7.cloned.1.call-update) | async-done | bytes 131088 | tf_op jit(solution)/shard_map/psum | solution.py:99
  763.9 0.9 select_add_fusion
  764.7 0.1 copy.53
  764.8 0.9 fusion.74
  765.7 11.7 %cholesky.16 = f32[128,128]{1,0:T(8,128)S(1)} custom-call(f32[128,128]{1,0:T(8,128)S(1)} %fusion.74), custom_call_target="Cholesky" | custom-call | tf_op jit(solution)/shard_map/jit(cholesky)/cholesky | solution.py:42
  777.4 0.6 compare_reduce_fusion
  778.1 0.7 fusion.69
  778.7 9.8 %custom-call.8 = f32[1,128,128]{1,2,0:T(8,128)S(1)} custom-call(f32[1,128,128]{2,1,0:T(8,128)S(1)} %fusion.69), custom_call_target="InvertDiagBlocksLowerTriangular" | custom-call | tf_op jit(solution)/shard_map/triangular_solve | solution.py:44
  788.5 1.1 fusion.72
  789.7 0.2 fusion.70
  789.9 0.5 fusion.30
  790.4 0.8 reduce.17
  791.2 0.1 reshape.215
  791.2 38.4 %all_to_all.65 = bf16[128,2,384]{2,1,0:T(2,128)(2,1)S(1)} all-to-all(bf16[128,2,384]{2,1,0:T(2,128)(2,1)S(1)} %reshape.215), channel_id=1, replica_groups=mesh['mem'=128,'rep'=4] {'mem'}, dimensions={0} | all-to-all | bytes 393216 | tf_op jit(solution)/shard_map/all_to_all | solution.py:109
  829.6 0.9 reshape.216
  (15 shorter events, 0.2 us)
Async XLA Ops:
  6.5 67.4 %copy-start = (bf16[384,1024]{1,0:T(8,128)(2,1)S(1)}, bf16[384,1024]{1,0:T(8,128)(2,1)}, u32[]{:S(2)}) copy-start(bf16[384,1024]{1,0:T(8,128)(2,1)} %param.14) | copy-start | bytes 2359300
  6.5 26.3 %copy-start.2 = (bf16[1,98304]{1,0:T(2,128)(2,1)S(1)}, bf16[1,98304]{1,0:T(2,128)(2,1)}, u32[]{:S(2)}) copy-start(bf16[1,98304]{1,0:T(2,128)(2,1)} %param.16) | copy-start | bytes 589828
  10.6 81.4 %all-to-all-start = ((bf16[128,2,384]{2,1,0:T(2,128)(2,1)}), bf16[128,2,384]{2,1,0:T(2,128)(2,1)}, u32[]{:S(2)}, u32[]{:S(2)}) async-start(bf16[128,2,384]{2,1,0:T(2,128)(2,1)} %reshape.213), calls=%async_computation | async-start | bytes 393216 | tf_op jit(solution)/shard_map/all_to_all | solution.py:104
  65.6 2.5 copy-start.1
  72.2 1.7 copy-start.5
  72.2 1.7 copy-start.6
  78.0 2.4 copy-start.3
  81.3 5.2 copy-start.4
  92.0 41.1 %all-to-all-start.1 = ((bf16[1,2,512,128]{3,1,0,2:T(2,128)(2,1)}), bf16[1,2,512,128]{3,1,0,2:T(2,128)(2,1)S(1)}, u32[]{:S(2)}, u32[]{:S(2)}) async-start(bf16[1,2,512,128]{3,1,0,2:T(2,128)(2,1)} %copy.44), calls=%async_computation.1 | async-start | bytes 524288 | tf_op jit(solution)/shard_map/all_to_all | solution.py:90
  133.1 271.2 %all-to-all-start.2 = ((bf16[1,2,512,128]{3,1,0,2:T(2,128)(2,1)}), bf16[1,2,512,128]{3,1,0,2:T(2,128)(2,1)S(1)}, u32[]{:S(2)}, u32[]{:S(2)}) async-start(bf16[1,2,512,128]{3,1,0,2:T(2,128)(2,1)} %copy.54), calls=%async_computation.2 | async-start | bytes 524288 | tf_op jit(solution)/shard_map/all_to_all | solution.py:91
  140.4 573.6 %all-reduce.5.cloned.1.call-start = ((), (), s32[]{:S(2)}) async-start(), calls=%async_computation.4 | async-start | bytes 262144 | tf_op jit(solution)/shard_map/psum | solution.py:100
  406.3 357.6 %all-reduce.7.cloned.1.call-start = ((), (), s32[]{:S(2)}) async-start(), calls=%async_computation.5 | async-start | bytes 262144 | tf_op jit(solution)/shard_map/psum | solution.py:99
Sparse Core Ops, SparseCore 0:
  406.4 307.5 all-reduce.4
  716.4 47.4 all-reduce.6
